TPU v7x, 128 devices: a whole 4x4x4 slice. The times are simulated.
128 devices in a mesh: row: 16 (over y, x), col: 8 (over z, core).
Axes of the slice: x: 4, y: 4, z: 4, core: 2. Of those that a mesh axis runs over, the one named last changes fastest.
Arguments:
- sample_counts: int32 [64], replicated, may hold values from 100 to 2000
- slot_silo: int32 [64], replicated, may hold values from 0 to 63, each once
- gate_weight: bfloat16 [28672, 8192], P('row', 'col'), may hold values from -3 to 3
- up_weight: bfloat16 [28672, 8192], P('row', 'col'), may hold values from -3 to 3
- down_weight: bfloat16 [8192, 28672], P('row', 'col'), may hold values from -3 to 3
- gate_a: bfloat16 [1024, 8192], P(('row', 'col')), may hold values from -6 to 6
- up_a: bfloat16 [1024, 8192], P(('row', 'col')), may hold values from -6 to 6
- down_a: bfloat16 [1024, 28672], P(('row', 'col')), may hold values from -6 to 6
- gate_b: bfloat16 [1024, 28672], P(('row', 'col')), may hold values from -6 to 6
- up_b: bfloat16 [1024, 28672], P(('row', 'col')), may hold values from -6 to 6
- down_b: bfloat16 [1024, 8192], P(('row', 'col')), may hold values from -6 to 6
Outputs:
- merged_gate: bfloat16 [28672, 8192], P('row', 'col')
- merged_up: bfloat16 [28672, 8192], P('row', 'col')
- merged_down: bfloat16 [8192, 28672], P('row', 'col')
Inputs may be any that keep to these rules, and one draw needn't show every extreme that they name: `slot_silo`: a permutation of the silos.
All inputs are finite; a program needn't handle non-finite values.
Results may differ from a plain program's by a relative error of at most 0.0043.
Values may be sent and summed in bfloat16 or wider, within the bound.
A program may use at most 128 MiB of HBM per device.

v0:
```python
import jax
import jax.numpy as jnp
from jax import lax
from jax.sharding import PartitionSpec as P

RANK = 16


def in_one_piece(arrays, axis, dim, along):
    ends, at = ([], 0)
    for a in arrays[:-1]:
        at += a.shape[along]
        ends.append(at)
    both = jnp.concatenate(arrays, axis=along)
    return tuple(jnp.split(lax.all_gather(both, axis, axis=dim, tiled=True), ends, axis=along))


def silo_scales(sample_counts, slot_silo, shard_rows):
    position = lax.axis_index(("row", "col"))
    row_ids = position * shard_rows + jnp.arange(shard_rows, dtype=jnp.int32)
    slot_ids = row_ids // RANK
    silo_table = jnp.arange(slot_silo.shape[0], dtype=jnp.int32)
    silo_ids = jnp.sum(
        jnp.where(slot_ids[:, None] == silo_table[None, :], slot_silo[None, :], 0), axis=1
    )
    counts_f = sample_counts.astype(jnp.float32)
    shares = counts_f / jnp.sum(counts_f)
    return jnp.sum(
        jnp.where(silo_ids[:, None] == silo_table[None, :], shares[None, :], 0.0), axis=1
    )


def local(
    sample_counts,
    slot_silo,
    gate_weight,
    up_weight,
    down_weight,
    gate_a,
    up_a,
    down_a,
    gate_b,
    up_b,
    down_b,
):
    shard_rows = gate_a.shape[0]
    n_row = lax.axis_size("row")
    n_col = lax.axis_size("col")
    row_scale = silo_scales(sample_counts, slot_silo, shard_rows)
    scaled_a = tuple(
        (
            (row_scale[:, None] * factor.astype(jnp.float32)).astype(jnp.bfloat16)
            for factor in (gate_a, up_a, down_a)
        )
    )
    weights = (gate_weight, up_weight, down_weight)
    spread_a = (
        lax.all_to_all(scaled_a[0], "col", split_axis=1, concat_axis=0, tiled=True),
        lax.all_to_all(scaled_a[1], "col", split_axis=1, concat_axis=0, tiled=True),
        lax.all_to_all(scaled_a[2], "col", split_axis=1, concat_axis=0, tiled=True),
    )
    spread_b = (
        lax.all_to_all(gate_b, "row", split_axis=1, concat_axis=0, tiled=True),
        lax.all_to_all(up_b, "row", split_axis=1, concat_axis=0, tiled=True),
        lax.all_to_all(down_b, "row", split_axis=1, concat_axis=0, tiled=True),
    )
    whole_b = in_one_piece((spread_b[0], spread_b[1], spread_b[2]), "col", 0, 1)
    stacked_b = tuple(
        (factor.reshape(n_col, n_row, shard_rows, factor.shape[1]) for factor in whole_b)
    )
    group_rows = n_col * shard_rows
    initial = tuple((jnp.zeros(weight.shape, jnp.float32) for weight in weights))
    pieces = in_one_piece((spread_a[0], spread_a[1], spread_a[2]), "row", 0, 1)
    results = []
    for running, factor_a, factor_b in zip(initial, pieces, stacked_b):
        groups = factor_a.shape[0] // group_rows
        grouped = factor_a.reshape(groups, n_col, shard_rows, factor_a.shape[1])
        results.append(
            jnp.einsum("jkrw,kjrv->wv", factor_b, grouped, preferred_element_type=jnp.float32)
        )
    updates = tuple(results)
    merged = tuple(
        (
            (weight.astype(jnp.float32) + update).astype(jnp.bfloat16)
            for weight, update in zip(weights, updates)
        )
    )
    return (merged[0], merged[1], merged[2])


def solution(mesh):
    return jax.shard_map(
        local,
        mesh=mesh,
        in_specs=(
            P(),
            P(),
            P("row", "col"),
            P("row", "col"),
            P("row", "col"),
            P(("row", "col"), None),
            P(("row", "col"), None),
            P(("row", "col"), None),
            P(("row", "col"), None),
            P(("row", "col"), None),
            P(("row", "col"), None),
        ),
        out_specs=(P("row", "col"), P("row", "col"), P("row", "col")),
        check_vma=False,
    )
```

profile of v0, /device:TPU:0, one launch (start us, length us, event | category | flops | bytes accessed | tf_op | source)
XLA Modules:
  0.0 225.7 jit_solution(16512068443444554002)
XLA Ops:
  7.2 0.0 copy-start.9
  7.2 0.0 copy-start.8
  7.2 0.0 copy-start.5
  7.2 0.0 copy-start.4
  7.2 0.0 copy-start.3
  7.2 0.0 all-gather.3.cloned.1.call-start
  7.3 15.3 %all_to_all.114 = bf16[8,16,512]{2,0,1:T(8,128)(2,1)S(1)} all-to-all(bf16[8,16,512]{2,0,1:T(8,128)(2,1)} %bitcast.67), channel_id=1, replica_groups=mesh['row'=16,'col'=8] {'row'}, dimensions={1} | all-to-all | bytes 262144 | tf_op jit(solution)/shard_map/all_to_all | solution.py:65
  22.5 13.3 %all_to_all.115 = bf16[8,16,1792]{2,0,1:T(8,128)(2,1)S(1)} all-to-all(bf16[8,16,1792]{2,0,1:T(8,128)(2,1)} %bitcast.65), channel_id=1, replica_groups=mesh['row'=16,'col'=8] {'row'}, dimensions={1} | all-to-all | bytes 917504 | tf_op jit(solution)/shard_map/all_to_all | solution.py:63
  35.8 13.3 %all_to_all.116 = bf16[8,16,1792]{2,0,1:T(8,128)(2,1)S(1)} all-to-all(bf16[8,16,1792]{2,0,1:T(8,128)(2,1)} %bitcast.66), channel_id=1, replica_groups=mesh['row'=16,'col'=8] {'row'}, dimensions={1} | all-to-all | bytes 917504 | tf_op jit(solution)/shard_map/all_to_all | solution.py:64
  49.1 1.1 pad_maximum_fusion
  50.1 0.0 all-gather.3.cloned.1.call-update
  50.2 0.0 copy-done.9
  50.2 0.6 convert_reduce_fusion
  50.8 0.0 copy-done.8
  50.8 0.2 select_reduce_fusion.1
  51.0 0.6 convert_divide_fusion
  51.6 0.2 select_reduce_fusion
  51.8 0.0 copy-done.5
  51.8 0.0 copy-done.4
  51.8 0.8 multiply_convert_fusion.2
  52.6 12.0 %all_to_all.117 = bf16[8,8,1024]{2,0,1:T(8,128)(2,1)S(1)} all-to-all(bf16[8,8,1024]{2,0,1:T(8,128)(2,1)S(1)} %bitcast.62), channel_id=1, replica_groups=mesh['row'=16,'col'=8] {'col'}, dimensions={1} | all-to-all | bytes 262144 | tf_op jit(solution)/shard_map/all_to_all | solution.py:59
  64.6 3.4 %all-to-all-start.3 = ((bf16[8,8,1024]{2,0,1:T(8,128)(2,1)}), bf16[8,8,1024]{2,0,1:T(8,128)(2,1)S(1)}, u32[]{:S(2)}, u32[]{:S(2)}) async-start(bf16[8,8,1024]{2,0,1:T(8,128)(2,1)} %bitcast.10), calls=%async_computation.3 | async-start | bytes 262144 | tf_op jit(solution)/shard_map/all_to_all | solution.py:58
  67.9 0.0 all-gather.5.cloned.1.call-start
  68.0 0.0 copy-done.3
  68.0 0.1 multiply_convert_fusion
  68.1 7.6 %all-to-all-done.3 = bf16[8,8,1024]{2,0,1:T(8,128)(2,1)S(1)} async-done(((bf16[8,8,1024]{2,0,1:T(8,128)(2,1)}), bf16[8,8,1024]{2,0,1:T(8,128)(2,1)S(1)}, u32[]{:S(2)}, u32[]{:S(2)}) %all-to-all-start.3) | async-done | bytes 131104 | tf_op jit(solution)/shard_map/all_to_all | solution.py:58
  75.8 17.3 %all_to_all.118 = bf16[8,8,3584]{2,0,1:T(8,128)(2,1)S(1)} all-to-all(bf16[8,8,3584]{2,0,1:T(8,128)(2,1)S(1)} %bitcast.57), channel_id=1, replica_groups=mesh['row'=16,'col'=8] {'col'}, dimensions={1} | all-to-all | bytes 917504 | tf_op jit(solution)/shard_map/all_to_all | solution.py:60
  93.1 0.9 pad_maximum_fusion.1
  94.1 0.0 all-gather.5.cloned.1.call-update
  94.1 11.3 %all-gather.3.cloned.1.call-done = bf16[1024,4096]{1,0:T(8,128)(2,1)} async-done(((bf16[128,4096]{1,0:T(8,128)(2,1)}), bf16[1024,4096]{1,0:T(8,128)(2,1)}) %all-gather.3.cloned.1.call-update) | async-done | bytes 8388624 | tf_op jit(solution)/shard_map/all_gather | solution.py:15
  105.4 6.7 %fusion.10 = (bf16[1024,1792]{1,0:T(8,128)(2,1)}, bf16[1024,1792]{1,0:T(8,128)(2,1)}) fusion(bf16[1024,4096]{1,0:T(8,128)(2,1)} %all-gather.3.cloned.1.call-done), kind=kLoop, calls=%fused_computation.26 | loop fusion | bytes 14680064 | tf_op jit(solution)/shard_map/split | solution.py:15
  112.1 0.0 slice-start.1
  112.1 79.8 %all-gather.5.cloned.1.call-done = bf16[1024,5632]{1,0:T(8,128)(2,1)} async-done(((bf16[64,5632]{1,0:T(8,128)(2,1)}), bf16[1024,5632]{1,0:T(8,128)(2,1)}) %all-gather.5.cloned.1.call-update) | async-done | bytes 11534352 | tf_op jit(solution)/shard_map/all_gather | solution.py:15
  191.9 0.0 slice-start
  191.9 0.0 slice-done.1
  191.9 3.1 %slice-done = bf16[1024,3584]{1,0:T(8,128)(2,1)S(1)} async-done(((bf16[1024,5632]{1,0:T(8,128)(2,1)}), bf16[1024,3584]{1,0:T(8,128)(2,1)S(1)}, s32[]{:S(2)}) %slice-start) | async-done | bytes 7340056 | tf_op jit(solution)/shard_map/split | solution.py:15
  195.0 7.1 %fusion = bf16[512,3584]{1,0:T(8,128)(2,1)} fusion(bf16[512,3584]{1,0:T(8,128)(2,1)} %param.15, bf16[8,16,8,512]{3,2,1,0:T(8,128)(2,1)S(1)} %bitcast.52, bf16[16,8,8,3584]{3,2,1,0:T(8,128)(2,1)S(1)} %bitcast.51), kind=kOutput, calls=%fused_computation.1 | convolution fusion | flops 3763601408 | bytes 15728640 | tf_op jit(solution)/shard_map/jkrw,kjrv->wv/dot_general | solution.py:79
  202.1 0.0 copy-start.1
  202.1 0.0 copy-start.6
  202.1 4.3 %fusion.9 = (bf16[1024,1024]{1,0:T(8,128)(2,1)S(1)}, bf16[1024,1024]{1,0:T(8,128)(2,1)}) fusion(bf16[1024,5632]{1,0:T(8,128)(2,1)} %all-gather.5.cloned.1.call-done), kind=kLoop, calls=%fused_computation.25 | loop fusion | bytes 8388608 | tf_op jit(solution)/shard_map/split | solution.py:15
  206.4 0.0 copy-done.1
  206.4 0.9 copy-done.6
  207.3 0.0 copy-start
  207.3 5.7 %fusion.1 = bf16[1792,1024]{1,0:T(8,128)(2,1)} fusion(bf16[1792,1024]{1,0:T(8,128)(2,1)S(1)} %copy-done.6, bf16[8,16,8,1792]{3,2,1,0:T(8,128)(2,1)S(1)} %bitcast.54, bf16[16,8,8,1024]{3,2,1,0:T(8,128)(2,1)S(1)} %bitcast.56), kind=kOutput, calls=%fused_computation.3 | convolution fusion | flops 3763601408 | bytes 13107200 | tf_op jit(solution)/shard_map/jkrw,kjrv->wv/dot_general | solution.py:79
  213.1 0.0 copy-done
  213.1 0.0 copy-done.2
  213.1 0.0 copy-done.7
  213.1 5.8 %fusion.2 = bf16[1792,1024]{1,0:T(8,128)(2,1)} fusion(bf16[1792,1024]{1,0:T(8,128)(2,1)S(1)} %copy-done.7, bf16[8,16,8,1792]{3,2,1,0:T(8,128)(2,1)S(1)} %bitcast.53, bf16[16,8,8,1024]{3,2,1,0:T(8,128)(2,1)S(1)} %bitcast.55), kind=kOutput, calls=%fused_computation.5 | convolution fusion | flops 3763601408 | bytes 13107200 | tf_op jit(solution)/shard_map/jkrw,kjrv->wv/dot_general | solution.py:79
  (3 shorter events, 0.0 us)
Async XLA Ops:
  7.2 43.0 %copy-start.9 = (s32[64]{0:T(128)S(1)}, s32[64]{0:T(128)}, u32[]{:S(2)}) copy-start(s32[64]{0:T(128)} %param.11) | copy-start | bytes 772
  7.2 43.6 %copy-start.8 = (s32[64]{0:T(128)S(1)}, s32[64]{0:T(128)}, u32[]{:S(2)}) copy-start(s32[64]{0:T(128)} %param.12) | copy-start | bytes 772
  7.2 44.6 %copy-start.5 = (bf16[8,8192]{1,0:T(8,128)(2,1)S(1)}, bf16[8,8192]{1,0:T(8,128)(2,1)}, u32[]{:S(2)}) copy-start(bf16[8,8192]{1,0:T(8,128)(2,1)} %param.17) | copy-start | bytes 393220
  7.2 44.6 %copy-start.4 = (bf16[8,8192]{1,0:T(8,128)(2,1)S(1)}, bf16[8,8192]{1,0:T(8,128)(2,1)}, u32[]{:S(2)}) copy-start(bf16[8,8192]{1,0:T(8,128)(2,1)} %param.16) | copy-start | bytes 393220
  7.2 60.8 %copy-start.3 = (bf16[8,28672]{1,0:T(8,128)(2,1)S(1)}, bf16[8,28672]{1,0:T(8,128)(2,1)}, u32[]{:S(2)}) copy-start(bf16[8,28672]{1,0:T(8,128)(2,1)} %param.18) | copy-start | bytes 1376260
  7.2 98.2 %all-gather.3.cloned.1.call-start = ((), (), s32[]{:S(2)}) async-start(), calls=%async_computation.6 | async-start | bytes 9437184 | tf_op jit(solution)/shard_map/all_gather | solution.py:15
  64.6 11.2 %all-to-all-start.3 = ((bf16[8,8,1024]{2,0,1:T(8,128)(2,1)}), bf16[8,8,1024]{2,0,1:T(8,128)(2,1)S(1)}, u32[]{:S(2)}, u32[]{:S(2)}) async-start(bf16[8,8,1024]{2,0,1:T(8,128)(2,1)} %bitcast.10), calls=%async_computation.3 | async-start | bytes 262144 | tf_op jit(solution)/shard_map/all_to_all | solution.py:58
  67.9 124.0 %all-gather.5.cloned.1.call-start = ((), (), s32[]{:S(2)}) async-start(), calls=%async_computation.7 | async-start | bytes 12255232 | tf_op jit(solution)/shard_map/all_gather | solution.py:15
  112.1 79.8 %slice-start.1 = ((bf16[1024,4096]{1,0:T(8,128)(2,1)}), bf16[1024,512]{1,0:T(8,128)(2,1)S(1)}, s32[]{:S(2)}) async-start(bf16[1024,4096]{1,0:T(8,128)(2,1)} %all-gather.3.cloned.1.call-done), calls=%async_computation.9 | async-start | bytes 2097152 | tf_op jit(solution)/shard_map/split | solution.py:15
  191.9 3.1 %slice-start = ((bf16[1024,5632]{1,0:T(8,128)(2,1)}), bf16[1024,3584]{1,0:T(8,128)(2,1)S(1)}, s32[]{:S(2)}) async-start(bf16[1024,5632]{1,0:T(8,128)(2,1)} %all-gather.5.cloned.1.call-done), calls=%async_computation.8 | async-start | bytes 14680064 | tf_op jit(solution)/shard_map/split | solution.py:15
  202.1 4.3 %copy-start.1 = (bf16[1024,1792]{1,0:T(8,128)(2,1)S(1)}, bf16[1024,1792]{1,0:T(8,128)(2,1)}, u32[]{:S(2)}) copy-start(bf16[1024,1792]{1,0:T(8,128)(2,1)} %get-tuple-element.5) | copy-start | bytes 11010052
  202.1 5.2 %copy-start.6 = (bf16[1792,1024]{1,0:T(8,128)(2,1)S(1)}, bf16[1792,1024]{1,0:T(8,128)(2,1)}, u32[]{:S(2)}) copy-start(bf16[1792,1024]{1,0:T(8,128)(2,1)} %param.14) | copy-start | bytes 11010052
  207.3 5.8 %copy-start = (bf16[1024,1792]{1,0:T(8,128)(2,1)S(1)}, bf16[1024,1792]{1,0:T(8,128)(2,1)}, u32[]{:S(2)}) copy-start(bf16[1024,1792]{1,0:T(8,128)(2,1)} %get-tuple-element.6) | copy-start | bytes 11010052
  207.3 5.8 %copy-start.2 = (bf16[1024,1024]{1,0:T(8,128)(2,1)S(1)}, bf16[1024,1024]{1,0:T(8,128)(2,1)}, u32[]{:S(2)}) copy-start(bf16[1024,1024]{1,0:T(8,128)(2,1)} %get-tuple-element.4) | copy-start | bytes 6291460
  207.3 5.8 %copy-start.7 = (bf16[1792,1024]{1,0:T(8,128)(2,1)S(1)}, bf16[1792,1024]{1,0:T(8,128)(2,1)}, u32[]{:S(2)}) copy-start(bf16[1792,1024]{1,0:T(8,128)(2,1)} %param.13) | copy-start | bytes 11010052
Sparse Core Ops, SparseCore 0:
  50.3 55.0 all-gather.2
  107.5 84.3 all-gather.4
where the time goes:
time: 227 us; the launch traced here: 226 us
  waiting for transfers between devices  98.8 us (44%)
  blocking collectives  71.1 us (31%)
  matrix products  18.7 us (8%)
  local copies, waits for them, and re-layouts  15 us (7%)
  between operations  14.2 us (6%)
  other arithmetic  4.54 us (2%)
  starting transfers between devices  3.45 us (2%)
    all_gather x2, waiting for transfers between devices, in_one_piece(): lax.all_gather(both, axis, axis=dim, tiled=True)  91.1 us
    dot_general x3, matrix products, local(): jnp.einsum('jkrw,kjrv->wv', factor_b, grouped, preferred_element_type=jnp...  18.7 us
    all_to_all x1, blocking collectives, local(): lax.all_to_all(scaled_a[2], 'col', split_axis=1, concat_axis=0, tiled=True)  17.3 us
    all_to_all x1, blocking collectives, local(): lax.all_to_all(down_b, 'row', split_axis=1, concat_axis=0, tiled=True)  15.3 us
    split x6, local copies, waits for them, and re-layouts, in_one_piece(): jnp.split(lax.all_gather(both, axis, axis=dim, tiled=True), ends, axis=al...  14.1 us
    all_to_all x1, blocking collectives, local(): lax.all_to_all(gate_b, 'row', split_axis=1, concat_axis=0, tiled=True)  13.3 us
    all_to_all x1, blocking collectives, local(): lax.all_to_all(up_b, 'row', split_axis=1, concat_axis=0, tiled=True)  13.3 us
    all_to_all x1, blocking collectives, local(): lax.all_to_all(scaled_a[1], 'col', split_axis=1, concat_axis=0, tiled=True)  12 us
  transfers between devices with their start and end apart: 3, of which 3 were waited for; matrix products, arithmetic and copies ran while one was open for 4% of the time, Pallas kernels for 0%

commit v1 on v0

v1 whole, which is shorter than its diff:
```python
import jax
import jax.numpy as jnp
from jax import lax
from jax.experimental import pallas as pl
from jax.experimental.pallas import tpu as pltpu
from jax.sharding import PartitionSpec as P

RANK = 16
MESH = pl.DeviceIdType.MESH
UNIT = 512
MB = 256


def kernel(
    counts_ref, slots_ref, gw, uw, dw, ga, ua, da, gb, ub, db,
    o0, o1, o2,
    abuf, bbuf, scaled, bt, scale,
    w_sem, a_send, a_recv, b_send, b_recv, z_send, z_recv, g_send, g_recv,
):
    ny, nx, nc, sub, _ = abuf.shape
    ranks = ny * nx * nc * sub
    row, col = lax.axis_index("row"), lax.axis_index("col")
    y, x = row // nx, lax.rem(row, nx)
    z, core = col // 2, lax.rem(col, 2)
    nz = nc // 2
    yp, ym = lax.rem(y + 1, ny), lax.rem(y + ny - 1, ny)
    xp, xm = lax.rem(x + 1, nx), lax.rem(x + nx - 1, nx)
    zp, zm, zo = (lax.rem(z + d, nz) for d in (1, nz - 1, 2))
    dev_xp, dev_xm = (y * nx + xp, col), (y * nx + xm, col)
    dev_yp, dev_ym = (yp * nx + x, col), (ym * nx + x, col)
    col_zp, col_zm, col_zo = zp * 2 + core, zm * 2 + core, zo * 2 + core
    dev_zp, dev_zm = (row, col_zp), (row, col_zm)
    mate = 1 - core
    dev_mate = (row, z * 2 + mate)

    barrier = pltpu.get_barrier_semaphore()
    col_peers = [lax.rem(col + k, nc) for k in range(1, nc)]
    row_peers = [
        lax.rem(y + dy, ny) * nx + lax.rem(x + dx, nx)
        for dy in range(ny)
        for dx in range(nx)
        if dy or dx
    ]
    for c in col_peers:
        pl.semaphore_signal(barrier, inc=1, device_id=(row, c), device_id_type=MESH)
    for r in row_peers:
        pl.semaphore_signal(barrier, inc=1, device_id=(r, col), device_id_type=MESH)
    pl.semaphore_wait(barrier, len(col_peers) + len(row_peers))

    started = []

    def send(src, dst, ssem, rsem, dev):
        copy = pltpu.make_async_remote_copy(
            src_ref=src, dst_ref=dst, send_sem=ssem, recv_sem=rsem,
            device_id=dev, device_id_type=MESH,
        )
        copy.start()
        started.append(copy)

    def arrived(ref, sem):
        pltpu.make_async_copy(ref, ref, sem).wait()

    a_parts = []
    at = 0
    for src in (ga, ua, da):
        n = src.shape[1] // nc
        a_parts.append((src, at, n))
        at += n
    b_parts = []
    at = 0
    for src in (gb, ub, db):
        n = src.shape[1] // (ny * nx)
        b_parts.append((src, at, n))
        at += n

    def spread_a(p):
        src, at, n = a_parts[p]
        for k, c in enumerate(col_peers):
            send(
                src.at[:, pl.ds(pl.multiple_of(c * n, n), n)],
                abuf.at[y, x, col, :, pl.ds(at, n)],
                a_send.at[p, k], a_recv.at[p], (row, c),
            )
        pltpu.make_async_copy(
            src.at[:, pl.ds(pl.multiple_of(col * n, n), n)],
            abuf.at[y, x, col, :, pl.ds(at, n)],
            a_recv.at[p],
        ).start()

    def spread_b(p):
        src, at, n = b_parts[p]
        for k, r in enumerate(row_peers):
            send(
                src.at[:, pl.ds(pl.multiple_of(r * n, n), n)],
                bbuf.at[y, x, col, :, pl.ds(at, n)],
                b_send.at[p, k], b_recv.at[p], (r, col),
            )
        pltpu.make_async_copy(
            src.at[:, pl.ds(pl.multiple_of(row * n, n), n)],
            bbuf.at[y, x, col, :, pl.ds(at, n)],
            b_recv.at[p],
        ).start()

    for p in range(3):
        spread_a(p)
        spread_b(p)
    outs = (o0, o1, o2)
    loads = [
        pltpu.make_async_copy(w, o, w_sem.at[i])
        for i, (w, o) in enumerate(zip((gw, uw, dw), outs))
    ]
    for load in loads:
        load.start()

    slots = slots_ref.shape[1]
    lane = lax.broadcasted_iota(jnp.int32, (ranks, slots), 1)
    slot = lax.broadcasted_iota(jnp.int32, (ranks, slots), 0) // RANK
    silo = jnp.sum(
        jnp.where(slot == lane, slots_ref[...].astype(jnp.float32), 0.0), axis=1, keepdims=True
    )
    counts = counts_ref[...].astype(jnp.float32)
    shares = counts / jnp.sum(counts, axis=1, keepdims=True)
    row_scale = jnp.sum(
        jnp.where(silo == lane.astype(jnp.float32), shares, 0.0), axis=1, keepdims=True
    )
    scale[...] = jnp.broadcast_to(row_scale, scale.shape)

    def b_block(p, ys, c):
        _, at, n = b_parts[p]
        return bbuf.at[ys, :, c, :, pl.ds(at, n)]

    whole, low, high = pl.ds(0, ny), pl.ds(0, ny // 2), pl.ds(ny // 2, ny // 2)

    def b_send_block(p, ys, c, k, dev):
        ref = b_block(p, ys, c)
        send(ref, ref, z_send.at[p, k], z_recv.at[p, k], dev)

    def zb1(p):
        arrived(b_block(p, whole, col), b_recv.at[p])
        b_send_block(p, whole, col, 0, dev_zp)
        b_send_block(p, whole, col, 1, dev_zm)
        b_send_block(p, whole, col, 4, dev_mate)

    def zb2(p):
        arrived(b_block(p, whole, col_zm), z_recv.at[p, 0])
        b_send_block(p, low, col_zm, 2, dev_zp)
        b_send_block(p, whole, col_zm, 5, dev_mate)
        arrived(b_block(p, whole, col_zp), z_recv.at[p, 1])
        b_send_block(p, high, col_zp, 3, dev_zm)
        b_send_block(p, whole, col_zp, 6, dev_mate)

    def zb3(p):
        arrived(b_block(p, low, col_zo), z_recv.at[p, 2])
        arrived(b_block(p, high, col_zo), z_recv.at[p, 3])
        b_send_block(p, whole, col_zo, 7, dev_mate)

    def b_done(p):
        for k, c in ((4, z), (5, zm), (6, zp), (7, zo)):
            arrived(b_block(p, whole, c * 2 + mate), z_recv.at[p, k])
        _, at, n = b_parts[p]

        def turn(m, carry):
            cols = pl.ds(pl.multiple_of(at + m * MB, MB), MB)
            bt[cols, :] = bbuf[:, :, :, :, cols].reshape(ranks, MB).T
            return carry

        lax.fori_loop(0, n // MB, turn, 0)

    half, quarter = nc // 2, nc // 4
    c_lo, c_hi = pl.ds(0, half), pl.ds(half, half)
    q0, q1, q2, q3 = (pl.ds(i * quarter, quarter) for i in range(4))
    every = pl.ds(0, nx)

    def a_ref(ys, xs, cs, u):
        return abuf.at[ys, xs, cs, :, pl.ds(u * UNIT, UNIT)]

    def move(u, d, ref, dev):
        send(ref, ref, g_send.at[u, d], g_recv.at[u, d], dev)

    def p1(u):
        for p, (_, at, n) in enumerate(a_parts):
            if at == u * UNIT:
                arrived(abuf.at[y, x, :, :, pl.ds(at, n)], a_recv.at[p])
        move(u, 0, a_ref(y, x, c_lo, u), dev_xp)
        move(u, 1, a_ref(y, x, c_lo, u), dev_xm)
        move(u, 2, a_ref(y, x, c_hi, u), dev_yp)
        move(u, 3, a_ref(y, x, c_hi, u), dev_ym)

    def r1(u):
        for d, ref, onward, dev in (
            (0, a_ref(y, xm, c_lo, u), a_ref(y, xm, q0, u), dev_xp),
            (1, a_ref(y, xp, c_lo, u), a_ref(y, xp, q1, u), dev_xm),
            (2, a_ref(ym, x, c_hi, u), a_ref(ym, x, q2, u), dev_yp),
            (3, a_ref(yp, x, c_hi, u), a_ref(yp, x, q3, u), dev_ym),
        ):
            arrived(ref, g_recv.at[u, d])
            move(u, 4 + d, onward, dev)

    xo, yo = lax.rem(x + 2, nx), lax.rem(y + 2, ny)

    def p2(u):
        arrived(a_ref(y, xo, q0, u), g_recv.at[u, 4])
        arrived(a_ref(y, xo, q1, u), g_recv.at[u, 5])
        move(u, 8, a_ref(y, every, c_lo, u), dev_yp)
        move(u, 9, a_ref(y, every, c_lo, u), dev_ym)
        arrived(a_ref(yo, x, q2, u), g_recv.at[u, 6])
        arrived(a_ref(yo, x, q3, u), g_recv.at[u, 7])
        move(u, 10, a_ref(whole, x, c_hi, u), dev_xp)
        move(u, 11, a_ref(whole, x, c_hi, u), dev_xm)

    def r2(u):
        for d, ref, onward, dev in (
            (8, a_ref(ym, every, c_lo, u), a_ref(ym, every, q0, u), dev_yp),
            (9, a_ref(yp, every, c_lo, u), a_ref(yp, every, q1, u), dev_ym),
            (10, a_ref(whole, xm, c_hi, u), a_ref(whole, xm, q2, u), dev_xp),
            (11, a_ref(whole, xp, c_hi, u), a_ref(whole, xp, q3, u), dev_xm),
        ):
            arrived(ref, g_recv.at[u, d])
            move(u, 4 + d, onward, dev)

    waited = set()

    def compute(u):
        arrived(a_ref(yo, every, q0, u), g_recv.at[u, 12])
        arrived(a_ref(yo, every, q1, u), g_recv.at[u, 13])
        arrived(a_ref(whole, xo, q2, u), g_recv.at[u, 14])
        arrived(a_ref(whole, xo, q3, u), g_recv.at[u, 15])
        p = max(i for i in range(3) if a_parts[i][1] <= u * UNIT)
        if p not in waited:
            waited.add(p)
            loads[p].wait()
        out = outs[p]
        ocols = pl.ds(u * UNIT - a_parts[p][1], UNIT)
        bat = b_parts[p][1]
        block = nc * sub

        def rescale(r, carry):
            rows = pl.ds(pl.multiple_of(r * block, block), block)
            a = abuf[r // nx, lax.rem(r, nx), :, :, pl.ds(u * UNIT, UNIT)]
            a = a.astype(jnp.float32).reshape(block, UNIT)
            s = scale[rows, :]
            s = jnp.concatenate([s] * (UNIT // s.shape[1]), axis=1)
            scaled[rows, :] = (a * s).astype(jnp.bfloat16)
            return carry

        lax.fori_loop(0, ny * nx, rescale, 0)

        def multiply(m, carry):
            orows = pl.ds(pl.multiple_of(m * MB, MB), MB)
            brows = pl.ds(pl.multiple_of(bat + m * MB, MB), MB)
            update = jnp.dot(bt[brows, :], scaled[...], preferred_element_type=jnp.float32)
            out[orows, ocols] = (out[orows, ocols].astype(jnp.float32) + update).astype(
                out.dtype
            )
            return carry

        lax.fori_loop(0, out.shape[0] // MB, multiply, 0)

    units = abuf.shape[4] // UNIT
    b_plan = {
        0: [(zb1, 0)],
        2: [(zb2, 0), (zb1, 1)],
        3: [(zb3, 0)],
        4: [(b_done, 0), (zb2, 1), (zb1, 2)],
        5: [(zb3, 1), (zb2, 2)],
        6: [(b_done, 1), (zb3, 2)],
        7: [(b_done, 2)],
    }
    c_plan = {5: [0], 6: [1], 7: [2], 8: [3, 4]}
    for u in range(5, units):
        c_plan[u + 4] = [u]
    for s in range(units + 4):
        for stage, lag in ((r2, 3), (p2, 2), (r1, 1), (p1, 0)):
            if 0 <= s - lag < units:
                stage(s - lag)
        for stage, p in b_plan.get(s, []):
            stage(p)
        for u in c_plan.get(s, []):
            compute(u)
    for copy in started:
        copy.wait_send()


def local(
    sample_counts, slot_silo, gate_weight, up_weight, down_weight,
    gate_a, up_a, down_a, gate_b, up_b, down_b,
):
    n_row, n_col = lax.axis_size("row"), lax.axis_size("col")
    ny = nx = 4
    sub = gate_a.shape[0]
    ranks = n_row * n_col * sub
    a_cols = sum(a.shape[1] // n_col for a in (gate_a, up_a, down_a))
    b_cols = sum(b.shape[1] // n_row for b in (gate_b, up_b, down_b))
    weights = (gate_weight, up_weight, down_weight)
    units = a_cols // UNIT
    dma = pltpu.SemaphoreType.DMA
    vmem = pl.BlockSpec(memory_space=pltpu.VMEM)
    hbm = pl.BlockSpec(memory_space=pltpu.HBM)
    return pl.pallas_call(
        kernel,
        out_shape=tuple(pltpu.VMEM(w.shape, w.dtype) for w in weights),
        in_specs=[vmem] * 2 + [hbm] * 9,
        out_specs=(vmem,) * 3,
        scratch_shapes=[
            pltpu.VMEM((ny, nx, n_col, sub, a_cols), jnp.bfloat16),
            pltpu.VMEM((ny, nx, n_col, sub, b_cols), jnp.bfloat16),
            pltpu.VMEM((ranks, UNIT), jnp.bfloat16),
            pltpu.VMEM((b_cols, ranks), jnp.bfloat16),
            pltpu.VMEM((ranks, 128), jnp.float32),
            dma((3,)),
            dma((3, n_col - 1)),
            dma((3,)),
            dma((3, n_row - 1)),
            dma((3,)),
            dma((3, 8)),
            dma((3, 8)),
            dma((units, 16)),
            dma((units, 16)),
        ],
        compiler_params=pltpu.CompilerParams(
            collective_id=0, has_side_effects=True, vmem_limit_bytes=50 * 1024 * 1024
        ),
    )(sample_counts.reshape(1, -1), slot_silo.reshape(1, -1), *weights,
      gate_a, up_a, down_a, gate_b, up_b, down_b)


def solution(mesh):
    spread, tile = P(("row", "col"), None), P("row", "col")
    return jax.shard_map(
        local,
        mesh=mesh,
        in_specs=(P(), P(), tile, tile, tile, spread, spread, spread, spread, spread, spread),
        out_specs=(tile, tile, tile),
        check_vma=False,
    )
```

time: 227 us -> 117 us (0.52)
  Pallas kernels: 0 us -> 111 us
  waiting for transfers between devices: 98.8 us -> 0 us
  blocking collectives: 71.1 us -> 0 us
  matrix products: 18.7 us -> 0 us
  between operations: 14.2 us -> 0.64 us
  local copies, waits for them, and re-layouts: 15 us -> 5.51 us
  other arithmetic: 4.54 us -> 0 us
  starting transfers between devices: 3.45 us -> 0 us
    pallas_call x0 -> x1, Pallas kernels: none -> 111 us  [local(): pl.pallas_call(kernel, out_shape=tuple((pltpu.VMEM(w.shape, w.dtype) for...]
    all_gather x2 -> x0, waiting for transfers between devices: 91.1 us -> none  [in_one_piece(): lax.all_gather(both, axis, axis=dim, tiled=True)]
    all_to_all x5 -> x0, blocking collectives: 71.1 us -> none  [the longest x1 17.3 us: local(): lax.all_to_all(scaled_a[2], 'col', split_axis=1, concat_axis=0, tiled=True)]
    dot_general x3 -> x0, matrix products: 18.7 us -> none  [local(): jnp.einsum('jkrw,kjrv->wv', factor_b, grouped, preferred_element_type=jnp...]
    split x6 -> x0, local copies, waits for them, and re-layouts: 14.1 us -> none  [in_one_piece(): jnp.split(lax.all_gather(both, axis, axis=dim, tiled=True), ends, axis=al...]
    all_to_all x1 -> x0, waiting for transfers between devices: 7.65 us -> none  [local(): lax.all_to_all(scaled_a[0], 'col', split_axis=1, concat_axis=0, tiled=True)]
    unnamed x20 -> x3, local copies, waits for them, and re-layouts: 0.93 us -> 5.51 us
    all_to_all x1 -> x0, starting transfers between devices: 3.37 us -> none  [local(): lax.all_to_all(scaled_a[0], 'col', split_axis=1, concat_axis=0, tiled=True)]
  transfers between devices with their start and end apart: 3 -> 0, of which waited for: 3 -> 0; matrix products, arithmetic and copies ran while one was open for 4% -> 0% of each run, Pallas kernels for 0% -> 0%
where the time goes in v1:
time: 117 us
  Pallas kernels  111 us (95%)
  local copies, waits for them, and re-layouts  5.51 us (5%)
    pallas_call x1, Pallas kernels, local(): pl.pallas_call(kernel, out_shape=tuple((pltpu.VMEM(w.shape, w.dtype) for...  111 us
    unnamed x3, local copies, waits for them, and re-layouts  5.51 us

profile of v1, /device:TPU:0, one launch (start us, length us, event | category | flops | bytes accessed | tf_op | source)
XLA Modules:
  0.0 116.7 jit_solution(17414237808716513647)
XLA Ops:
  0.6 110.6 %shard_map.130 = (bf16[1792,1024]{1,0:T(8,128)(2,1)S(1)}, bf16[1792,1024]{1,0:T(8,128)(2,1)S(1)}, bf16[512,3584]{1,0:T(8,128)(2,1)S(1)}) custom-call(s32[1,64]{1,0:T(1,128)} %bitcast.2, s32[1,64]{1,0:T(1,128)} %bitcast.3, bf16[1792,1024]{1,0:T(8,128)(2,1)} %gw.1, bf16[1792,1024]{1,0:T(8,128)(2,1)} %uw.1, bf16[512,3584]{1,0:T(8,128)(2,1)} %dw.1, ...), custom_call_target="tpu_custom_call" | custom-call | tf_op jit(solution)/shard_map/pallas_call | solution.py:299
  111.2 1.8 %copy.17 = bf16[1792,1024]{1,0:T(8,128)(2,1)} copy(bf16[1792,1024]{1,0:T(8,128)(2,1)S(1)} %get-tuple-element.3) | data formatting | bytes 7340032
  113.1 1.8 %copy.18 = bf16[1792,1024]{1,0:T(8,128)(2,1)} copy(bf16[1792,1024]{1,0:T(8,128)(2,1)S(1)} %get-tuple-element.4) | data formatting | bytes 7340032
  114.9 1.8 %copy.19 = bf16[512,3584]{1,0:T(8,128)(2,1)} copy(bf16[512,3584]{1,0:T(8,128)(2,1)S(1)} %get-tuple-element.5) | data formatting | bytes 7340032

commit v2 on v1

v2 whole, which is shorter than its diff:
```python
import jax
import jax.numpy as jnp
from jax import lax
from jax.experimental import pallas as pl
from jax.experimental.pallas import tpu as pltpu
from jax.sharding import PartitionSpec as P

RANK = 16
MESH = pl.DeviceIdType.MESH
UNIT = 256
WIDE = 512
TALL = 896
LAG = (0, 2, 4, 6, 8)
WINDOW = 8


def kernel(
    counts_hbm, slots_hbm, gw, uw, dw, ga, ua, da, gb, ub, db,
    o0, o1, o2,
    abuf, bbuf, scaled, scale, counts_ref, slots_ref,
    s_sem, w_sem, sent, a_recv, b_recv, z_recv, g_recv,
):
    ny, nx, nc, sub, _ = abuf.shape
    ranks = ny * nx * nc * sub
    row, col = lax.axis_index("row"), lax.axis_index("col")
    y, x = row // nx, lax.rem(row, nx)
    z, core = col // 2, lax.rem(col, 2)
    nz = nc // 2
    yp, ym = lax.rem(y + 1, ny), lax.rem(y + ny - 1, ny)
    xp, xm = lax.rem(x + 1, nx), lax.rem(x + nx - 1, nx)
    zp, zm, zo = (lax.rem(z + d, nz) for d in (1, nz - 1, 2))
    dev_xp, dev_xm = (y * nx + xp, col), (y * nx + xm, col)
    dev_yp, dev_ym = (yp * nx + x, col), (ym * nx + x, col)
    col_zp, col_zm, col_zo = zp * 2 + core, zm * 2 + core, zo * 2 + core
    dev_zp, dev_zm = (row, col_zp), (row, col_zm)
    mate = 1 - core
    dev_mate = (row, z * 2 + mate)

    small = [
        pltpu.make_async_copy(h, v, s_sem.at[i])
        for i, (h, v) in enumerate(((counts_hbm, counts_ref), (slots_hbm, slots_ref)))
    ]
    for copy in small:
        copy.start()
    barrier = pltpu.get_barrier_semaphore()
    col_peers = [lax.rem(col + k, nc) for k in range(1, nc)]
    row_peers = [
        lax.rem(y + dy, ny) * nx + lax.rem(x + dx, nx)
        for dy in range(ny)
        for dx in range(nx)
        if dy or dx
    ]
    for c in col_peers:
        pl.semaphore_signal(barrier, inc=1, device_id=(row, c), device_id_type=MESH)
    for r in row_peers:
        pl.semaphore_signal(barrier, inc=1, device_id=(r, col), device_id_type=MESH)
    pl.semaphore_wait(barrier, len(col_peers) + len(row_peers))

    def send(src, dst, kind, rsem, dev):
        pltpu.make_async_remote_copy(
            src_ref=src, dst_ref=dst, send_sem=sent.at[kind], recv_sem=rsem,
            device_id=dev, device_id_type=MESH,
        ).start()

    def arrived(ref, sem):
        pltpu.make_async_copy(ref, ref, sem).wait()

    a_parts = []
    at = 0
    for src in (ga, ua, da):
        n = src.shape[1] // nc
        a_parts.append((src, at, n))
        at += n
    b_parts, b_start = [], []
    at = 0
    for src in (gb, ub, db):
        total = src.shape[1] // (ny * nx)
        b_start.append(at)
        n = min(total, TALL)
        for begin in range(0, total, n):
            b_parts.append((src, total, begin, at + begin, n))
        at += total

    def spread_a(p):
        src, at, n = a_parts[p]
        for c in col_peers:
            send(
                src.at[:, pl.ds(pl.multiple_of(c * n, n), n)],
                abuf.at[y, x, col, :, pl.ds(at, n)],
                0, a_recv.at[p], (row, c),
            )
        pltpu.make_async_copy(
            src.at[:, pl.ds(pl.multiple_of(col * n, n), n)],
            abuf.at[y, x, col, :, pl.ds(at, n)],
            a_recv.at[p],
        ).start()

    def spread_b(p):
        src, total, begin, at, n = b_parts[p]
        for r in row_peers:
            send(
                src.at[:, pl.ds(pl.multiple_of(r * total + begin, 128), n)],
                bbuf.at[y, x, col, :, pl.ds(at, n)],
                1, b_recv.at[p], (r, col),
            )
        pltpu.make_async_copy(
            src.at[:, pl.ds(pl.multiple_of(row * total + begin, 128), n)],
            bbuf.at[y, x, col, :, pl.ds(at, n)],
            b_recv.at[p],
        ).start()

    for p in range(3):
        spread_a(p)
        if p < 2:
            spread_b(p)
    outs = (o0, o1, o2)
    loads = [
        pltpu.make_async_copy(w, o, w_sem.at[i])
        for i, (w, o) in enumerate(zip((gw, uw, dw), outs))
    ]
    for load in loads:
        load.start()

    for copy in small:
        copy.wait()
    slots = slots_ref.shape[1]
    lane = lax.broadcasted_iota(jnp.int32, (ranks, slots), 1)
    slot = lax.broadcasted_iota(jnp.int32, (ranks, slots), 0) // RANK
    silo = jnp.sum(
        jnp.where(slot == lane, slots_ref[...].astype(jnp.float32), 0.0), axis=1, keepdims=True
    )
    counts = counts_ref[...].astype(jnp.float32)
    shares = counts / jnp.sum(counts, axis=1, keepdims=True)
    row_scale = jnp.sum(
        jnp.where(silo == lane.astype(jnp.float32), shares, 0.0), axis=1, keepdims=True
    )
    scale[...] = jnp.broadcast_to(row_scale, scale.shape)

    def b_block(p, ys, c):
        _, _, _, at, n = b_parts[p]
        return bbuf.at[ys, :, c, :, pl.ds(at, n)]

    whole, low, high = pl.ds(0, ny), pl.ds(0, ny // 2), pl.ds(ny // 2, ny // 2)

    def b_send_block(p, ys, c, k, dev):
        ref = b_block(p, ys, c)
        send(ref, ref, 2, z_recv.at[p, k], dev)

    def zb1(p):
        arrived(b_block(p, whole, col), b_recv.at[p])
        b_send_block(p, whole, col, 0, dev_zp)
        b_send_block(p, whole, col, 1, dev_zm)
        b_send_block(p, whole, col, 3, dev_mate)

    def zb2(p):
        arrived(b_block(p, whole, col_zm), z_recv.at[p, 0])
        b_send_block(p, low, col_zm, 2, dev_zp)
        b_send_block(p, whole, col_zm, 3, dev_mate)
        arrived(b_block(p, whole, col_zp), z_recv.at[p, 1])
        b_send_block(p, high, col_zp, 2, dev_zm)
        b_send_block(p, whole, col_zp, 3, dev_mate)

    def zb3(p):
        arrived(b_block(p, whole, col_zo), z_recv.at[p, 2])
        b_send_block(p, whole, col_zo, 3, dev_mate)

    def b_done(p):
        _, _, _, at, n = b_parts[p]
        arrived(bbuf.at[:, :, pl.ds(0, nz), :, pl.ds(at, n)], z_recv.at[p, 3])

    half, quarter = nc // 2, nc // 4
    c_lo, c_hi = pl.ds(0, half), pl.ds(half, half)
    q0, q1, q2, q3 = (pl.ds(i * quarter, quarter) for i in range(4))
    every = pl.ds(0, nx)

    def a_ref(ys, xs, cs, u):
        return abuf.at[ys, xs, cs, :, pl.ds(u * UNIT, UNIT)]

    def move(u, d, ref, dev):
        send(ref, ref, 3, g_recv.at[u % WINDOW, d], dev)

    def p1(u):
        for p, (_, at, n) in enumerate(a_parts):
            if at == u * UNIT:
                arrived(abuf.at[y, x, :, :, pl.ds(at, n)], a_recv.at[p])
        move(u, 0, a_ref(y, x, c_lo, u), dev_xp)
        move(u, 1, a_ref(y, x, c_lo, u), dev_xm)
        move(u, 2, a_ref(y, x, c_hi, u), dev_yp)
        move(u, 3, a_ref(y, x, c_hi, u), dev_ym)

    def r1(u):
        for d, ref, onward, dev in (
            (0, a_ref(y, xm, c_lo, u), a_ref(y, xm, q0, u), dev_xp),
            (1, a_ref(y, xp, c_lo, u), a_ref(y, xp, q1, u), dev_xm),
            (2, a_ref(ym, x, c_hi, u), a_ref(ym, x, q2, u), dev_yp),
            (3, a_ref(yp, x, c_hi, u), a_ref(yp, x, q3, u), dev_ym),
        ):
            arrived(ref, g_recv.at[u % WINDOW, d])
            move(u, 4, onward, dev)

    def p2(u):
        arrived(a_ref(y, x, pl.ds(0, nc), u), g_recv.at[u % WINDOW, 4])
        move(u, 5, a_ref(y, every, c_lo, u), dev_yp)
        move(u, 6, a_ref(y, every, c_lo, u), dev_ym)
        move(u, 7, a_ref(whole, x, c_hi, u), dev_xp)
        move(u, 8, a_ref(whole, x, c_hi, u), dev_xm)

    def r2(u):
        for d, ref, onward, dev in (
            (5, a_ref(ym, every, c_lo, u), a_ref(ym, every, q0, u), dev_yp),
            (6, a_ref(yp, every, c_lo, u), a_ref(yp, every, q1, u), dev_ym),
            (7, a_ref(whole, xm, c_hi, u), a_ref(whole, xm, q2, u), dev_xp),
            (8, a_ref(whole, xp, c_hi, u), a_ref(whole, xp, q3, u), dev_xm),
        ):
            arrived(ref, g_recv.at[u % WINDOW, d])
            move(u, 9, onward, dev)

    flat = bbuf.reshape(ranks, bbuf.shape[4])
    block = nc * sub
    waited = set()

    def complete(u):
        arrived(a_ref(y, every, pl.ds(0, nc), u), g_recv.at[u % WINDOW, 9])

    def compute(us, m):
        begin, n = us[0] * UNIT, len(us) * UNIT
        p = part_of(us[0])
        if p not in waited:
            waited.add(p)
            loads[p].wait()
        out = outs[p]
        ocols = pl.ds(begin - a_parts[p][1], n)

        def rescale(r, carry):
            rows = pl.ds(pl.multiple_of(r * block, block), block)
            a = abuf[r // nx, lax.rem(r, nx), :, :, pl.ds(begin, n)]
            a = a.astype(jnp.float32).reshape(block, n)
            s = scale[rows, :]
            s = jnp.concatenate([s] * (n // s.shape[1]), axis=1)
            scaled[rows, pl.ds(0, n)] = (a * s).astype(jnp.bfloat16)
            return carry

        if m == 0:
            lax.fori_loop(0, ny * nx, rescale, 0)
        tall = min(out.shape[0], TALL)
        orows = pl.ds(m * tall, tall)
        update = lax.dot_general(
            flat[:, pl.ds(b_start[p] + m * tall, tall)],
            scaled[:, pl.ds(0, n)],
            (((0,), (0,)), ((), ())),
            preferred_element_type=jnp.float32,
        )
        out[orows, ocols] = (out[orows, ocols].astype(jnp.float32) + update).astype(
            out.dtype
        )

    def part_of(u):
        return max(i for i in range(3) if a_parts[i][1] <= u * UNIT)

    units = abuf.shape[4] // UNIT
    b_plan = {
        0: [(zb1, 0), (spread_b, 2)],
        1: [(zb1, 1), (spread_b, 3)],
        2: [(spread_b, 4)],
        4: [(zb2, 0), (zb1, 2)],
        7: [(zb3, 0), (zb2, 1), (zb1, 3)],
        10: [(zb3, 1), (zb2, 2), (zb1, 4)],
        11: [(b_done, 0), (b_done, 1)],
        13: [(zb3, 2), (zb2, 3)],
        15: [(zb3, 3), (zb2, 4)],
        17: [(zb3, 4), (b_done, 2), (b_done, 3)],
        18: [(b_done, 4)],
    }
    ready = {0: 12, 1: 17, 2: 19}
    wide = WIDE // UNIT
    work = []
    for u in range(0, units, wide):
        p = part_of(u)
        tiles = max(1, outs[p].shape[0] // TALL)
        if u + wide < units:
            work += [(list(range(u, u + wide)), m, ready[p]) for m in range(tiles)]
        else:
            work += [([v], m, 0) for v in range(u, units) for m in range(tiles)]
    c_plan, step = {}, 0
    for us, m, least in work:
        step = max(step + 1, us[-1] + LAG[4], least)
        c_plan.setdefault(min(step, units - 1 + LAG[4]), []).append((us, m))
    for s in range(units + LAG[4]):
        for stage, lag in (
            (r2, LAG[3]), (p2, LAG[2]), (r1, LAG[1]), (p1, LAG[0]), (complete, LAG[4])
        ):
            if 0 <= s - lag < units:
                stage(s - lag)
        for stage, p in b_plan.get(s, []):
            stage(p)
        for us, m in c_plan.get(s, []):
            compute(us, m)
    af = abuf.reshape(ny * nx * nc, sub, abuf.shape[4])
    bf = bbuf.reshape(ny * nx * nc, sub, bbuf.shape[4])
    a_count, b_count = ny * nx * nc, ny * nx
    arrived(af.at[pl.ds(0, nc - 1)], sent.at[0])
    arrived(bf.at[pl.ds(0, b_count - 1)], sent.at[1])
    arrived(bf.at[pl.ds(0, 7 * b_count)], sent.at[2])
    arrived(af.at[pl.ds(0, a_count - nc)], sent.at[3])


def local(
    sample_counts, slot_silo, gate_weight, up_weight, down_weight,
    gate_a, up_a, down_a, gate_b, up_b, down_b,
):
    n_row, n_col = lax.axis_size("row"), lax.axis_size("col")
    ny = nx = 4
    sub = gate_a.shape[0]
    ranks = n_row * n_col * sub
    a_cols = sum(a.shape[1] // n_col for a in (gate_a, up_a, down_a))
    b_cols = sum(b.shape[1] // n_row for b in (gate_b, up_b, down_b))
    weights = (gate_weight, up_weight, down_weight)
    pieces = sum(
        max(1, b.shape[1] // n_row // TALL) for b in (gate_b, up_b, down_b)
    )
    dma = pltpu.SemaphoreType.DMA
    vmem = pl.BlockSpec(memory_space=pltpu.VMEM)
    hbm = pl.BlockSpec(memory_space=pltpu.HBM)
    return pl.pallas_call(
        kernel,
        out_shape=tuple(pltpu.VMEM(w.shape, w.dtype) for w in weights),
        in_specs=[hbm] * 11,
        out_specs=(vmem,) * 3,
        scratch_shapes=[
            pltpu.VMEM((ny, nx, n_col, sub, a_cols), jnp.bfloat16),
            pltpu.VMEM((ny, nx, n_col, sub, b_cols), jnp.bfloat16),
            pltpu.VMEM((ranks, WIDE), jnp.bfloat16),
            pltpu.VMEM((ranks, 128), jnp.float32),
            pltpu.VMEM((1, sample_counts.shape[0]), jnp.int32),
            pltpu.VMEM((1, slot_silo.shape[0]), jnp.int32),
            dma((2,)),
            dma((3,)),
            dma((4,)),
            dma((3,)),
            dma((pieces,)),
            dma((pieces, 4)),
            dma((WINDOW, 10)),
        ],
        compiler_params=pltpu.CompilerParams(
            collective_id=0, has_side_effects=True, vmem_limit_bytes=50 * 1024 * 1024
        ),
    )(sample_counts.reshape(1, -1), slot_silo.reshape(1, -1), *weights,
      gate_a, up_a, down_a, gate_b, up_b, down_b)


def solution(mesh):
    spread, tile = P(("row", "col"), None), P("row", "col")
    return jax.shard_map(
        local,
        mesh=mesh,
        in_specs=(P(), P(), tile, tile, tile, spread, spread, spread, spread, spread, spread),
        out_specs=(tile, tile, tile),
        check_vma=False,
    )
```

time: 117 us -> 91.9 us (0.79)
  Pallas kernels: 111 us -> 85.6 us
    pallas_call x1, Pallas kernels: 111 us -> 85.6 us  [local(): pl.pallas_call(kernel, out_shape=tuple((pltpu.VMEM(w.shape, w.dtype) for...]
where the time goes in v2:
time: 91.9 us; the launch traced here: 91.8 us
  Pallas kernels  85.6 us (93%)
  local copies, waits for them, and re-layouts  5.51 us (6%)
    pallas_call x1, Pallas kernels, local(): pl.pallas_call(kernel, out_shape=tuple((pltpu.VMEM(w.shape, w.dtype) for...  85.6 us
    unnamed x3, local copies, waits for them, and re-layouts  5.51 us

profile of v2, /device:TPU:0, one launch (start us, length us, event | category | flops | bytes accessed | tf_op | source)
XLA Modules:
  0.0 91.8 jit_solution(9468659930286062231)
XLA Ops:
  0.6 85.6 %shard_map.130 = (bf16[1792,1024]{1,0:T(8,128)(2,1)S(1)}, bf16[1792,1024]{1,0:T(8,128)(2,1)S(1)}, bf16[512,3584]{1,0:T(8,128)(2,1)S(1)}) custom-call(s32[1,64]{1,0:T(1,128)} %bitcast.2, s32[1,64]{1,0:T(1,128)} %bitcast.3, bf16[1792,1024]{1,0:T(8,128)(2,1)} %gw.1, bf16[1792,1024]{1,0:T(8,128)(2,1)} %uw.1, bf16[512,3584]{1,0:T(8,128)(2,1)} %dw.1, ...), custom_call_target="tpu_custom_call" | custom-call | tf_op jit(solution)/shard_map/pallas_call | solution.py:324
  86.3 1.8 %copy.17 = bf16[1792,1024]{1,0:T(8,128)(2,1)} copy(bf16[1792,1024]{1,0:T(8,128)(2,1)S(1)} %get-tuple-element.3) | data formatting | bytes 7340032
  88.1 1.8 %copy.18 = bf16[1792,1024]{1,0:T(8,128)(2,1)} copy(bf16[1792,1024]{1,0:T(8,128)(2,1)S(1)} %get-tuple-element.4) | data formatting | bytes 7340032
  89.9 1.8 %copy.19 = bf16[512,3584]{1,0:T(8,128)(2,1)} copy(bf16[512,3584]{1,0:T(8,128)(2,1)S(1)} %get-tuple-element.5) | data formatting | bytes 7340032

commit v3 on v2

--- a/solution.py
+++ b/solution.py
@@ -10,8 +10,10 @@
 UNIT = 256
 WIDE = 512
 TALL = 896
-LAG = (0, 2, 4, 6, 8)
-WINDOW = 8
+LAG = (0, 2, 4, 5, 7)
+AHEAD = 90
+WINDOW = 10
+PARTS = 4
 
 
 def kernel(
@@ -46,9 +48,9 @@
     col_peers = [lax.rem(col + k, nc) for k in range(1, nc)]
     row_peers = [
         lax.rem(y + dy, ny) * nx + lax.rem(x + dx, nx)
-        for dy in range(ny)
-        for dx in range(nx)
-        if dy or dx
+        for dy, dx in (
+            (2, 2), (0, 1), (1, 0), (0, 3), (3, 0), (1, 2), (2, 1), (3, 2), (2, 3), (1, 1), (3, 3), (1, 3), (3, 1), (0, 2), (2, 0)
+        )
     ]
     for c in col_peers:
         pl.semaphore_signal(barrier, inc=1, device_id=(row, c), device_id_type=MESH)
@@ -81,16 +83,21 @@
             b_parts.append((src, total, begin, at + begin, n))
         at += total
 
+    a_pieces = []
+    for src, at, n in a_parts:
+        cuts = [0, UNIT, n] if at == 0 else [0, n]
+        a_pieces += [(src, n, b, at + b, e - b) for b, e in zip(cuts, cuts[1:])]
+
     def spread_a(p):
-        src, at, n = a_parts[p]
+        src, total, begin, at, n = a_pieces[p]
         for c in col_peers:
             send(
-                src.at[:, pl.ds(pl.multiple_of(c * n, n), n)],
+                src.at[:, pl.ds(pl.multiple_of(c * total + begin, 128), n)],
                 abuf.at[y, x, col, :, pl.ds(at, n)],
                 0, a_recv.at[p], (row, c),
             )
         pltpu.make_async_copy(
-            src.at[:, pl.ds(pl.multiple_of(col * n, n), n)],
+            src.at[:, pl.ds(pl.multiple_of(col * total + begin, 128), n)],
             abuf.at[y, x, col, :, pl.ds(at, n)],
             a_recv.at[p],
         ).start()
@@ -109,7 +116,7 @@
             b_recv.at[p],
         ).start()
 
-    for p in range(3):
+    for p in range(len(a_pieces)):
         spread_a(p)
         if p < 2:
             spread_b(p)
@@ -180,7 +187,7 @@
         send(ref, ref, 3, g_recv.at[u % WINDOW, d], dev)
 
     def p1(u):
-        for p, (_, at, n) in enumerate(a_parts):
+        for p, (_, _, _, at, n) in enumerate(a_pieces):
             if at == u * UNIT:
                 arrived(abuf.at[y, x, :, :, pl.ds(at, n)], a_recv.at[p])
         move(u, 0, a_ref(y, x, c_lo, u), dev_xp)
@@ -283,14 +290,20 @@
             work += [([v], m, 0) for v in range(u, units) for m in range(tiles)]
     c_plan, step = {}, 0
     for us, m, least in work:
-        step = max(step + 1, us[-1] + LAG[4], least)
-        c_plan.setdefault(min(step, units - 1 + LAG[4]), []).append((us, m))
+        step = max(step + 1, 2 * (us[-1] + LAG[4]), 2 * least)
+        c_plan.setdefault(min(step // 2, units - 1 + LAG[4]), []).append((us, m))
+    order = (
+        (p2, lambda u: u * AHEAD // 100 + LAG[2]),
+        (r1, lambda u: u * AHEAD // 100 + LAG[1]),
+        (p1, lambda u: u * AHEAD // 100 + LAG[0]),
+        (r2, lambda u: u + LAG[3]),
+        (complete, lambda u: u + LAG[4]),
+    )
     for s in range(units + LAG[4]):
-        for stage, lag in (
-            (r2, LAG[3]), (p2, LAG[2]), (r1, LAG[1]), (p1, LAG[0]), (complete, LAG[4])
-        ):
-            if 0 <= s - lag < units:
-                stage(s - lag)
+        for stage, when in order:
+            for u in range(units):
+                if when(u) == s:
+                    stage(u)
         for stage, p in b_plan.get(s, []):
             stage(p)
         for us, m in c_plan.get(s, []):
@@ -302,6 +315,19 @@
     arrived(bf.at[pl.ds(0, b_count - 1)], sent.at[1])
     arrived(bf.at[pl.ds(0, 7 * b_count)], sent.at[2])
     arrived(af.at[pl.ds(0, a_count - nc)], sent.at[3])
+
+
+def write_out(i0, i1, i2, o0, o1, o2, sem):
+    copies = []
+    for k, (i, o) in enumerate(((i0, o0), (i1, o1), (i2, o2))):
+        n = i.shape[0] // PARTS
+        for m in range(PARTS):
+            rows = pl.ds(m * n, n)
+            copies.append(pltpu.make_async_copy(i.at[rows], o.at[rows], sem.at[k, m]))
+    for copy in copies:
+        copy.start()
+    for copy in copies:
+        copy.wait()
 
 
 def local(
@@ -321,7 +347,7 @@
     dma = pltpu.SemaphoreType.DMA
     vmem = pl.BlockSpec(memory_space=pltpu.VMEM)
     hbm = pl.BlockSpec(memory_space=pltpu.HBM)
-    return pl.pallas_call(
+    results = pl.pallas_call(
         kernel,
         out_shape=tuple(pltpu.VMEM(w.shape, w.dtype) for w in weights),
         in_specs=[hbm] * 11,
@@ -336,7 +362,7 @@
             dma((2,)),
             dma((3,)),
             dma((4,)),
-            dma((3,)),
+            dma((4,)),
             dma((pieces,)),
             dma((pieces, 4)),
             dma((WINDOW, 10)),
@@ -346,6 +372,15 @@
         ),
     )(sample_counts.reshape(1, -1), slot_silo.reshape(1, -1), *weights,
       gate_a, up_a, down_a, gate_b, up_b, down_b)
+    anywhere = pl.BlockSpec(memory_space=pl.ANY)
+    return pl.pallas_call(
+        write_out,
+        out_shape=tuple(jax.ShapeDtypeStruct(w.shape, w.dtype) for w in weights),
+        in_specs=[anywhere] * 3,
+        out_specs=(hbm,) * 3,
+        scratch_shapes=[dma((3, PARTS))],
+        compiler_params=pltpu.CompilerParams(vmem_limit_bytes=2 * 1024 * 1024),
+    )(*results)
 
 
 def solution(mesh):

time: 91.9 us -> 90.7 us (0.987)
  local copies, waits for them, and re-layouts: 5.51 us -> 0 us
  Pallas kernels: 85.6 us -> 89.8 us
    unnamed x3 -> x0, local copies, waits for them, and re-layouts: 5.51 us -> none
    pallas_call x0 -> x1, Pallas kernels: none -> 4.2 us  [local(): pl.pallas_call(write_out, out_shape=tuple((jax.ShapeDtypeStruct(w.shape,...]
where the time goes in v3:
time: 90.7 us; the launch traced here: 90.6 us
  Pallas kernels  89.8 us (99%)
    pallas_call x1, Pallas kernels, local(): pl.pallas_call(kernel, out_shape=tuple((pltpu.VMEM(w.shape, w.dtype) for...  85.6 us
    pallas_call x1, Pallas kernels, local(): pl.pallas_call(write_out, out_shape=tuple((jax.ShapeDtypeStruct(w.shape,...  4.2 us

profile of v3, /device:TPU:0, one launch (start us, length us, event | category | flops | bytes accessed | tf_op | source)
XLA Modules:
  0.0 90.6 jit_solution(9073368317406876439)
XLA Ops:
  0.6 85.6 %shard_map.130 = (bf16[1792,1024]{1,0:T(8,128)(2,1)S(1)}, bf16[1792,1024]{1,0:T(8,128)(2,1)S(1)}, bf16[512,3584]{1,0:T(8,128)(2,1)S(1)}) custom-call(s32[1,64]{1,0:T(1,128)} %bitcast.2, s32[1,64]{1,0:T(1,128)} %bitcast.3, bf16[1792,1024]{1,0:T(8,128)(2,1)} %gw.1, bf16[1792,1024]{1,0:T(8,128)(2,1)} %uw.1, bf16[512,3584]{1,0:T(8,128)(2,1)} %dw.1, ...), custom_call_target="tpu_custom_call" | custom-call | tf_op jit(solution)/shard_map/pallas_call | solution.py:350
  86.2 4.2 %shard_map.131 = (bf16[1792,1024]{1,0:T(8,128)(2,1)}, bf16[1792,1024]{1,0:T(8,128)(2,1)}, bf16[512,3584]{1,0:T(8,128)(2,1)}) custom-call(bf16[1792,1024]{1,0:T(8,128)(2,1)S(1)} %get-tuple-element.6.i0, bf16[1792,1024]{1,0:T(8,128)(2,1)S(1)} %get-tuple-element.7.i1, bf16[512,3584]{1,0:T(8,128)(2,1)S(1)} %get-tuple-element.8.i2), custom_call_target="tpu_custom_call" | custom-call | tf_op jit(solution)/shard_map/pallas_call | solution.py:376
